TPU v7x, 32 devices: a whole 2x2x4 slice. The times are simulated.
32 devices in a mesh: leaf: 16 (over z, y, x), col: 2 (over core).
Axes of the slice: x: 2, y: 2, z: 4, core: 2. Of those that a mesh axis runs over, the one named last changes fastest.
Arguments:
- sources: bfloat16 [65536, 256], P('leaf', 'col'), may hold values from -6 to 6
- near_tiles: bfloat16 [256, 8, 256, 256], P('leaf', 'col'), may hold values from -0.125 to 0.125
- near_index: int32 [256, 8], P('leaf'), may hold values from 0 to 255, as said below
- near_count: int32 [256], P('leaf'), may hold values from 1 to 8, as said below
- leaf_basis: bfloat16 [256, 64, 256], P('leaf'), may hold values from -0.375 to 0.375
- leaf_coupling: bfloat16 [256, 64, 256], P('leaf'), may hold values from -0.375 to 0.375
- leaf_far: int32 [256, 4], P('leaf'), may hold values from 0 to 255, as said below
- up_leaf: bfloat16 [32, 64, 512], P('leaf'), may hold values from -0.25 to 0.25
- mid_coupling: bfloat16 [32, 64, 256], P('leaf'), may hold values from -0.375 to 0.375
- mid_far: int32 [32, 4], P('leaf'), may hold values from 0 to 31, as said below
- up_mid: bfloat16 [32, 64, 64], P('leaf'), may hold values from -0.75 to 0.75
- top_coupling: bfloat16 [4, 64, 256], replicated, may hold values from -0.4375 to 0.4375
Outputs:
- product: float32 [65536, 256], P('leaf', 'col')
Inputs may be any that keep to these rules, and one draw needn't show every extreme that they name: `near_index`: entry 0 of row i is i; the other 7 entries are distinct leaves j with j != i and |i - j| <= 8. Only the first near_count[i] slots of leaf i count; some leaf has all 8. `leaf_far`: row i holds 4 distinct leaves j != i with |i // 8 - j // 8| <= 1. `mid_far`: row a holds 4 distinct middle clusters b != a with |a // 8 - b // 8| <= 1.
All inputs are finite; a program needn't handle non-finite values.
Results may differ from a plain program's by a relative error of at most 0.01.
Values may be sent and summed in bfloat16 or wider, within the bound.
No kernel may reach another device: no remote copies, remote signals or barrier semaphores. Data moves between devices by JAX's collectives and lax.ppermute only.
A program may use at most 128 MiB of HBM per device.

v0:
```python
import jax
import jax.numpy as jnp
from jax import lax
from jax.sharding import PartitionSpec as P

CHILD = 8
FAR = 4


def padded(x, sides, width):
    for axis, dim in sides:
        size, length = (lax.axis_size(axis), x.shape[dim])
        up = [(i, (i + 1) % size) for i in range(size - 1)]
        down = [(j, i) for i, j in up]
        last = lax.slice_in_dim(x, length - width, length, axis=dim)
        first = lax.slice_in_dim(x, 0, width, axis=dim)
        before = lax.ppermute(last, axis, up)
        after = lax.ppermute(first, axis, down)
        x = jnp.concatenate([before, x, after], axis=dim)
    return x


def shards(
    sources,
    near_tiles,
    near_index,
    near_count,
    leaf_basis,
    leaf_coupling,
    leaf_far,
    up_leaf,
    mid_coupling,
    mid_far,
    up_mid,
    top_coupling,
):
    f32 = jnp.float32
    bf16 = jnp.bfloat16
    leaf_count = leaf_basis.shape[0]
    rank_size = leaf_basis.shape[1]
    leaf_size = leaf_basis.shape[2]
    col_count = sources.shape[1]
    mid_count = leaf_count // CHILD
    total_top = top_coupling.shape[0]
    device = lax.axis_index("leaf")
    first_leaf = device * leaf_count
    first_mid = device * mid_count
    window = padded(sources, (("leaf", 0),), CHILD * leaf_size)
    near_local = near_index - (first_leaf - CHILD)
    all_tiles = lax.all_gather(near_tiles, "col", axis=1, tiled=True)
    slot_count = all_tiles.shape[1]
    blocks = window.reshape(-1, leaf_size, window.shape[1])
    picked = blocks[near_local]
    live_mask = jnp.arange(slot_count)[None, :] < near_count[:, None]
    picked = jnp.where(live_mask[:, :, None, None], picked, jnp.zeros((), bf16))
    result = jnp.einsum("lsij,lsjc->lic", all_tiles, picked, preferred_element_type=f32)
    near_part = result.reshape(leaf_count * leaf_size, window.shape[1])
    leaf_blocks = sources.reshape(leaf_count, leaf_size, col_count)
    leaf_coef = jnp.einsum(
        "lrk,lkc->lrc", leaf_basis, leaf_blocks, preferred_element_type=f32
    ).astype(bf16)
    mid_coef = jnp.einsum(
        "qrk,qkc->qrc",
        up_leaf,
        leaf_coef.reshape(mid_count, CHILD * rank_size, col_count),
        preferred_element_type=f32,
    ).astype(bf16)
    mid_lift = jnp.einsum("qrs,qsc->qrc", up_mid, mid_coef, preferred_element_type=f32).astype(bf16)
    parent = (first_mid + jnp.arange(mid_count)) // CHILD
    mid_flat = mid_far.reshape(-1)
    top_range = jnp.arange(total_top)
    coef_piece = lax.all_gather(mid_coef, "leaf", axis=0, tiled=True)
    lift_piece = lax.all_gather(mid_lift, "leaf", axis=0, tiled=True)
    global_ids = jnp.arange(coef_piece.shape[0])
    group_map = (top_range[:, None] == (global_ids // CHILD)[None, :]).astype(bf16)
    top_total = jnp.einsum("pk,krc->prc", group_map, lift_piece, preferred_element_type=f32)
    global_ids = jnp.arange(coef_piece.shape[0])
    pick_map = (mid_flat[:, None] == global_ids[None, :]).astype(bf16)
    mid_picked = jnp.einsum("ik,krc->irc", pick_map, coef_piece, preferred_element_type=f32)
    top_coef = top_total.astype(bf16)
    parent_rows = top_coupling[parent]
    keep_mask = top_range[None, :] != parent[:, None]
    stacked = jnp.where(keep_mask[:, :, None, None], top_coef[None], jnp.zeros((), bf16))
    top_field = jnp.einsum(
        "qrk,qkc->qrc",
        parent_rows,
        stacked.reshape(mid_count, total_top * rank_size, col_count),
        preferred_element_type=f32,
    ).astype(bf16)
    mid_chosen = mid_picked.astype(bf16).reshape(mid_count, FAR * rank_size, col_count)
    mid_field = (
        jnp.einsum("qrk,qkc->qrc", mid_coupling, mid_chosen, preferred_element_type=f32)
        + jnp.einsum("qrs,qrc->qsc", up_mid, top_field, preferred_element_type=f32)
    ).astype(bf16)
    leaf_window = padded(leaf_coef, (("leaf", 0),), CHILD)
    far_local = leaf_far - (first_leaf - CHILD)
    leaf_chosen = leaf_window[far_local].reshape(leaf_count, FAR * rank_size, col_count)
    down_part = jnp.einsum("qrs,qrc->qsc", up_leaf, mid_field, preferred_element_type=f32).reshape(
        leaf_count, rank_size, col_count
    )
    leaf_field = (
        jnp.einsum("lrk,lkc->lrc", leaf_coupling, leaf_chosen, preferred_element_type=f32)
        + down_part
    ).astype(bf16)
    far_part = jnp.einsum(
        "lrk,lrc->lkc", leaf_basis, leaf_field, preferred_element_type=f32
    ).reshape(leaf_count * leaf_size, col_count)
    return near_part + far_part


def solution(mesh):
    return jax.shard_map(
        shards,
        mesh=mesh,
        in_specs=(
            P("leaf", "col"),
            P("leaf", "col", None, None),
            P("leaf", None),
            P("leaf"),
            P("leaf", None, None),
            P("leaf", None, None),
            P("leaf", None),
            P("leaf", None, None),
            P("leaf", None, None),
            P("leaf", None),
            P("leaf", None, None),
            P(),
        ),
        out_specs=P("leaf", "col"),
        check_vma=False,
    )
```

profile of v0, /device:TPU:0, one launch (start us, length us, event | category | flops | bytes accessed | tf_op | source)
XLA Modules:
  0.0 168.7 jit_solution(13844385451105794318)
XLA Ops:
  6.5 0.0 copy-start
  6.5 0.0 copy-start.1
  6.5 0.0 all-gather.2.cloned.1.call-start
  6.5 0.7 all-gather.2.cloned.1.call-update
  7.3 0.0 copy-start.9
  7.3 0.0 copy-start.4
  7.3 0.0 copy-start.6
  7.3 0.0 copy-start.11
  7.3 0.0 copy-start.7
  7.3 0.0 copy-start.10
  7.3 0.0 copy-start.8
  7.3 0.0 copy-start.5
  7.3 0.2 copy-done
  7.6 0.3 copy-done.1
  7.9 0.3 convolution_convert_fusion
  8.3 4.9 %collective-permute-start.2 = (bf16[8,64,128]{2,1,0:T(8,128)(2,1)S(1)}, bf16[8,64,128]{2,1,0:T(8,128)(2,1)S(1)}, u32[]{:S(2)}, u32[]{:S(2)}) collective-permute-start(bf16[8,64,128]{2,1,0:T(8,128)(2,1)S(1)} %get-tuple-element.7), channel_id=1, source_target_pairs={{0,2},{2,4},{4,6},{6,8},{8,10},{10,12},{12,14},{14,16},{16,18},{18... | collective-permute-start | bytes 393224 | tf_op jit(solution)/shard_map/ppermute | solution.py:17
  13.2 1.3 collective-permute-start.3
  14.5 1.1 fusion.33
  15.5 5.4 %collective-permute-start = (bf16[2048,128]{1,0:T(8,128)(2,1)}, bf16[2048,128]{1,0:T(8,128)(2,1)}, u32[]{:S(2)}, u32[]{:S(2)}) collective-permute-start(bf16[2048,128]{1,0:T(8,128)(2,1)} %get-tuple-element.5), channel_id=1, source_target_pairs={{0,2},{2,4},{4,6},{6,8},{8,10},{10,12},{12,14},{14,16},{16,18},{18... | collective-permute-start | bytes 1572872 | tf_op jit(solution)/shard_map/ppermute | solution.py:17
  20.9 1.3 collective-permute-start.1
  22.2 0.0 copy-done.9
  22.2 0.1 copy.27
  22.3 0.1 reshape.160
  22.4 0.0 copy-done.4
  22.4 0.2 convolution_convert_fusion.5
  22.6 0.0 copy-done.6
  22.6 0.1 fusion.12
  22.7 0.0 copy-start.3
  22.7 57.8 %all_gather.11 = bf16[32,64,128]{2,1,0:T(8,128)(2,1)S(1)} all-gather(bf16[2,64,128]{2,1,0:T(8,128)(2,1)S(1)} %fusion.12), channel_id=1, replica_groups=mesh['leaf'=16,'col'=2] {'leaf'}, dimensions={0}, use_global_device_ids=true | all-gather | bytes 557056 | tf_op jit(solution)/shard_map/all_gather | solution.py:73
  80.5 0.4 convolution_convert_fusion.2
  80.9 0.1 iota_compare_fusion.3
  81.0 0.1 broadcast_in_dim.59
  81.1 0.1 broadcast_in_dim.60
  81.2 0.0 copy-done.11
  81.2 0.1 eq.28
  81.3 38.7 %all_gather.10 = bf16[32,64,128]{2,1,0:T(8,128)(2,1)S(1)} all-gather(bf16[2,64,128]{2,1,0:T(8,128)(2,1)S(1)} %bitcast.59), channel_id=1, replica_groups=mesh['leaf'=16,'col'=2] {'leaf'}, dimensions={0}, use_global_device_ids=true | all-gather | bytes 557056 | tf_op jit(solution)/shard_map/all_gather | solution.py:72
  119.9 0.4 convolution_convert_fusion.1
  120.4 0.0 copy-done.7
  120.4 0.6 gather_fusion.2
  121.0 0.0 copy-done.10
  121.0 0.1 iota_compare_fusion
  121.1 0.0 copy-done.8
  121.1 0.4 fusion.11
  121.5 0.0 copy-done.5
  121.5 0.4 convolution_bitcast_fusion.1
  121.9 0.1 copy.25
  122.0 0.1 reshape.152
  122.1 0.2 copy.33
  122.3 0.0 collective-permute-done.2
  122.3 0.0 collective-permute-done.3
  122.3 1.0 pad_maximum_fusion.1
  123.3 0.7 gather_fusion.1
  124.0 0.0 copy-done.3
  124.0 1.9 %fusion.9 = f32[16,128,256]{2,1,0:T(8,128)} fusion(bf16[16,64,256]{2,1,0:T(8,128)(2,1)S(1)} %copy-done, f32[16,64,128]{2,1,0:T(8,128)S(1)} %bitcast.57, bf16[16,64,256]{2,1,0:T(8,128)(2,1)S(1)} %copy-done.3, bf16[16,256,128]{2,1,0:T(8,128)(2,1)S(1)} %bitcast.56), kind=kOutput, calls=%fused_computation.15 | convolution fusion | flops 134479872 | bytes 4718592 | tf_op jit(solution)/shard_map/lrk,lrc->lkc/dot_general | solution.py:105
  126.0 0.0 collective-permute-done
  126.0 0.0 collective-permute-done.1
  126.0 1.7 pad_maximum_fusion
  127.6 6.6 %gather_fusion = bf16[128,256,128]{2,1,0:T(8,128)(2,1)} fusion(bf16[32,256,128]{2,1,0:T(8,128)(2,1)S(1)} %bitcast.52, s32[1024]{0:T(1024)S(1)} %pad_clamp_fusion.2), kind=kCustom, calls=%fused_computation | custom fusion | bytes 16777728 | tf_op jit(solution)/shard_map/gather | solution.py:53
  134.2 0.0 copy-start.2
  134.2 12.1 %copy.26 = bf16[128,256,128]{1,2,0:T(8,128)(2,1)} copy(bf16[128,256,128]{2,1,0:T(8,128)(2,1)} %gather_fusion) | data formatting | bytes 16777216 | tf_op jit(solution)/shard_map/gather | solution.py:53
  146.3 0.0 all-gather.2.cloned.1.call-done
  146.3 0.0 copy-done.2
  146.3 12.7 %fusion.4 = f32[16,256,128]{1,2,0:T(8,128)} fusion(f32[16,128,256]{2,1,0:T(8,128)S(1)} %copy-done.2, bf16[16,8,256,256]{3,2,1,0:T(8,128)(2,1)} %all-gather.2.cloned.1.call-done, bf16[16,8,256,128]{2,3,1,0:T(8,128)(2,1)} %bitcast.54, pred[16,8]{1,0:T(8,128)(4,1)S(1)} %iota_compare_fusion), kind=kOutput, calls=%fused_computation.9 | convolution fusion | flops 2152202240 | bytes 29360256 | tf_op jit(solution)/shard_map/lsij,lsjc->lic/dot_general | solution.py:56
  159.0 2.9 %copy.34 = f32[16,256,128]{2,1,0:T(8,128)} copy(f32[16,256,128]{1,2,0:T(8,128)} %fusion.4) | data formatting | bytes 4194304 | tf_op jit(solution)/shard_map/add | solution.py:108
  (11 shorter events, 0.1 us)
Async XLA Ops:
  6.5 1.0 copy-start
  6.5 1.4 copy-start.1
  6.5 139.8 %all-gather.2.cloned.1.call-start = ((), (), s32[]{:S(2)}) async-start(), calls=%async_computation | async-start | bytes 25165824 | tf_op jit(solution)/shard_map/all_gather | solution.py:50
  7.3 14.9 %copy-start.9 = (s32[16,4]{0,1:T(4,128)S(1)}, s32[16,4]{0,1:T(4,128)}, u32[]{:S(2)}) copy-start(s32[16,4]{0,1:T(4,128)} %param.18) | copy-start | bytes 772
  7.3 15.1 %copy-start.4 = (bf16[2,64,512]{2,1,0:T(8,128)(2,1)S(1)}, bf16[2,64,512]{2,1,0:T(8,128)(2,1)}, u32[]{:S(2)}) copy-start(bf16[2,64,512]{2,1,0:T(8,128)(2,1)} %param.19) | copy-start | bytes 393220
  7.3 15.3 %copy-start.6 = (bf16[2,64,64]{2,1,0:T(8,128)(2,1)S(1)}, bf16[2,64,64]{2,1,0:T(8,128)(2,1)}, u32[]{:S(2)}) copy-start(bf16[2,64,64]{2,1,0:T(8,128)(2,1)} %param.22) | copy-start | bytes 49156
  7.3 73.9 %copy-start.11 = (s32[2,4]{1,0:T(2,128)S(1)}, s32[2,4]{1,0:T(2,128)}, u32[]{:S(2)}) copy-start(s32[2,4]{1,0:T(2,128)} %param.21) | copy-start | bytes 100
  7.3 113.1 %copy-start.7 = (bf16[4,64,256]{2,1,0:T(8,128)(2,1)S(1)}, bf16[4,64,256]{2,1,0:T(8,128)(2,1)}, u32[]{:S(2)}) copy-start(bf16[4,64,256]{2,1,0:T(8,128)(2,1)} %param.23) | copy-start | bytes 393220
  7.3 113.7 %copy-start.10 = (s32[16]{0:T(128)S(1)}, s32[16]{0:T(128)}, u32[]{:S(2)}) copy-start(s32[16]{0:T(128)} %param.15) | copy-start | bytes 196
  7.3 113.7 %copy-start.8 = (s32[16,8]{0,1:T(8,128)S(1)}, s32[16,8]{0,1:T(8,128)}, u32[]{:S(2)}) copy-start(s32[16,8]{0,1:T(8,128)} %param.14) | copy-start | bytes 1540
  7.3 114.1 %copy-start.5 = (bf16[2,64,256]{2,1,0:T(8,128)(2,1)S(1)}, bf16[2,64,256]{2,1,0:T(8,128)(2,1)}, u32[]{:S(2)}) copy-start(bf16[2,64,256]{2,1,0:T(8,128)(2,1)} %param.20) | copy-start | bytes 196612
  8.3 114.0 %collective-permute-start.2 = (bf16[8,64,128]{2,1,0:T(8,128)(2,1)S(1)}, bf16[8,64,128]{2,1,0:T(8,128)(2,1)S(1)}, u32[]{:S(2)}, u32[]{:S(2)}) collective-permute-start(bf16[8,64,128]{2,1,0:T(8,128)(2,1)S(1)} %get-tuple-element.7), channel_id=1, source_target_pairs={{0,2},{2,4},{4,6},{6,8},{8,10},{10,12},{12,14},{14,16},{16,18},{18... | collective-permute-start | bytes 393224 | tf_op jit(solution)/shard_map/ppermute | solution.py:17
  13.2 109.1 %collective-permute-start.3 = (bf16[8,64,128]{2,1,0:T(8,128)(2,1)S(1)}, bf16[8,64,128]{2,1,0:T(8,128)(2,1)}, u32[]{:S(2)}, u32[]{:S(2)}) collective-permute-start(bf16[8,64,128]{2,1,0:T(8,128)(2,1)S(1)} %get-tuple-element.8), channel_id=1, source_target_pairs={{2,0},{4,2},{6,4},{8,6},{10,8},{12,10},{14,12},{16,14},{18,16},{20... | collective-permute-start | bytes 393224 | tf_op jit(solution)/shard_map/ppermute | solution.py:18
  15.5 110.4 %collective-permute-start = (bf16[2048,128]{1,0:T(8,128)(2,1)}, bf16[2048,128]{1,0:T(8,128)(2,1)}, u32[]{:S(2)}, u32[]{:S(2)}) collective-permute-start(bf16[2048,128]{1,0:T(8,128)(2,1)} %get-tuple-element.5), channel_id=1, source_target_pairs={{0,2},{2,4},{4,6},{6,8},{8,10},{10,12},{12,14},{14,16},{16,18},{18... | collective-permute-start | bytes 1572872 | tf_op jit(solution)/shard_map/ppermute | solution.py:17
  20.9 105.1 %collective-permute-start.1 = (bf16[2048,128]{1,0:T(8,128)(2,1)}, bf16[2048,128]{1,0:T(8,128)(2,1)}, u32[]{:S(2)}, u32[]{:S(2)}) collective-permute-start(bf16[2048,128]{1,0:T(8,128)(2,1)} %get-tuple-element.6), channel_id=1, source_target_pairs={{2,0},{4,2},{6,4},{8,6},{10,8},{12,10},{14,12},{16,14},{18,16},{20... | collective-permute-start | bytes 1572872 | tf_op jit(solution)/shard_map/ppermute | solution.py:18
  22.7 101.3 %copy-start.3 = (bf16[16,64,256]{2,1,0:T(8,128)(2,1)S(1)}, bf16[16,64,256]{2,1,0:T(8,128)(2,1)}, u32[]{:S(2)}) copy-start(bf16[16,64,256]{2,1,0:T(8,128)(2,1)} %param.17) | copy-start | bytes 1572868
  134.2 12.1 %copy-start.2 = (f32[16,128,256]{2,1,0:T(8,128)S(1)}, f32[16,128,256]{2,1,0:T(8,128)}, u32[]{:S(2)}) copy-start(f32[16,128,256]{2,1,0:T(8,128)} %fusion.9) | copy-start | bytes 6291460
Sparse Core Ops, SparseCore 0:
  8.9 32.7 all-gather.1
where the time goes:
time: 169 us
  blocking collectives  96.5 us (57%)
  local copies, waits for them, and re-layouts  25.4 us (15%)
  matrix products  16.8 us (10%)
  between operations  13.7 us (8%)
  starting transfers between devices  12.8 us (8%)
  other arithmetic  2.82 us (2%)
    all_gather x1, blocking collectives, shards(): lift_piece = lax.all_gather(mid_lift, 'leaf', axis=0, tiled=True)  57.8 us
    all_gather x1, blocking collectives, shards(): coef_piece = lax.all_gather(mid_coef, 'leaf', axis=0, tiled=True)  38.7 us
    gather x2, local copies, waits for them, and re-layouts, shards(): picked = blocks[near_local]  18.7 us
    dot_general x1, matrix products, shards(): jnp.einsum('lsij,lsjc->lic', all_tiles, picked, preferred_element_type=f32)  12.7 us
    ppermute x2, starting transfers between devices, padded(): before = lax.ppermute(last, axis, up)  10.2 us
  transfers between devices with their start and end apart: 5, of which 0 were waited for; matrix products, arithmetic and copies ran while one was open for 17% of the time, Pallas kernels for 0%

commit v1 on v0

--- a/solution.py
+++ b/solution.py
@@ -5,6 +5,22 @@
 
 CHILD = 8
 FAR = 4
+
+
+def summed_both_ways(shard, axis, dim, term):
+    peers, position, span = (lax.axis_size(axis), lax.axis_index(axis), shard.shape[dim])
+    right = [(i, (i + 1) % peers) for i in range(peers)]
+    left = [(i, (i - 1) % peers) for i in range(peers)]
+    halfway = peers // 2
+    from_left = from_right = shard
+    total = term(shard, position * span)
+    for step in range(1, halfway + 1):
+        from_left = lax.ppermute(from_left, axis, right)
+        if step < peers - halfway:
+            from_right = lax.ppermute(from_right, axis, left)
+            total = total + term(from_right, (position + step) % peers * span)
+        total = total + term(from_left, (position - step) % peers * span)
+    return total
 
 
 def padded(x, sides, width):
@@ -70,10 +86,19 @@
     mid_flat = mid_far.reshape(-1)
     top_range = jnp.arange(total_top)
     coef_piece = lax.all_gather(mid_coef, "leaf", axis=0, tiled=True)
-    lift_piece = lax.all_gather(mid_lift, "leaf", axis=0, tiled=True)
     global_ids = jnp.arange(coef_piece.shape[0])
     group_map = (top_range[:, None] == (global_ids // CHILD)[None, :]).astype(bf16)
-    top_total = jnp.einsum("pk,krc->prc", group_map, lift_piece, preferred_element_type=f32)
+    top_total = summed_both_ways(
+        mid_lift,
+        "leaf",
+        0,
+        lambda own_block, start: jnp.einsum(
+            "pk,krc->prc",
+            lax.dynamic_slice_in_dim(group_map, start, own_block.shape[0], axis=1),
+            own_block,
+            preferred_element_type=f32,
+        ),
+    )
     global_ids = jnp.arange(coef_piece.shape[0])
     pick_map = (mid_flat[:, None] == global_ids[None, :]).astype(bf16)
     mid_picked = jnp.einsum("ik,krc->irc", pick_map, coef_piece, preferred_element_type=f32)

time: 169 us -> 195 us (1.15)
  blocking collectives: 96.5 us -> 49.3 us
  waiting for transfers between devices: 0.72 us -> 33.3 us
  starting transfers between devices: 12.8 us -> 42.8 us
  matrix products: 16.8 us -> 24.1 us
    all_gather x1 -> x0, blocking collectives: 57.8 us -> none  [shards(): lift_piece = lax.all_gather(mid_lift, 'leaf', axis=0, tiled=True)]
    ppermute x0 -> x15, starting transfers between devices: none -> 33.5 us  [the longest x7 26.7 us: summed_both_ways(): from_right = lax.ppermute(from_right, axis, left)]
    ppermute x0 -> x15, waiting for transfers between devices: none -> 32.6 us  [the longest x8 24.1 us: summed_both_ways(): from_left = lax.ppermute(from_left, axis, right)]
    all_gather x1, blocking collectives: 38.7 us -> 49.3 us  [shards(): coef_piece = lax.all_gather(mid_coef, 'leaf', axis=0, tiled=True)]
    dot_general x1 -> x16, matrix products: 0.4 us -> 6.03 us  [shards(): jnp.einsum('pk,krc->prc', lax.dynamic_slice_in_dim(group_map, start, own_...]
    ppermute x2, starting transfers between devices: 10.2 us -> 6.63 us  [padded(): before = lax.ppermute(last, axis, up)]
  transfers between devices with their start and end apart: 5 -> 20, of which waited for: 0 -> 9; matrix products, arithmetic and copies ran while one was open for 17% -> 20% of each run, Pallas kernels for 0% -> 0%
where the time goes in v1:
time: 195 us; the launch traced here: 194 us
  blocking collectives  49.3 us (25%)
  starting transfers between devices  42.8 us (22%)
  waiting for transfers between devices  33.3 us (17%)
  local copies, waits for them, and re-layouts  27.2 us (14%)
  matrix products  24.1 us (12%)
  between operations  14.1 us (7%)
  other arithmetic  2.97 us (2%)
    all_gather x1, blocking collectives, shards(): coef_piece = lax.all_gather(mid_coef, 'leaf', axis=0, tiled=True)  49.3 us
    ppermute x7, starting transfers between devices, summed_both_ways(): from_right = lax.ppermute(from_right, axis, left)  26.7 us
    ppermute x8, waiting for transfers between devices, summed_both_ways(): from_left = lax.ppermute(from_left, axis, right)  24.1 us
    gather x2, local copies, waits for them, and re-layouts, shards(): picked = blocks[near_local]  18.7 us
    dot_general x1, matrix products, shards(): jnp.einsum('lsij,lsjc->lic', all_tiles, picked, preferred_element_type=f32)  12.7 us
    ppermute x7, waiting for transfers between devices, summed_both_ways(): from_right = lax.ppermute(from_right, axis, left)  8.5 us
    ppermute x8, starting transfers between devices, summed_both_ways(): from_left = lax.ppermute(from_left, axis, right)  6.83 us
    ppermute x2, starting transfers between devices, padded(): before = lax.ppermute(last, axis, up)  6.63 us
  transfers between devices with their start and end apart: 20, of which 9 were waited for; matrix products, arithmetic and copies ran while one was open for 20% of the time, Pallas kernels for 0%

profile of v1, /device:TPU:0, one launch (start us, length us, event | category | flops | bytes accessed | tf_op | source)
XLA Modules:
  0.0 193.8 jit_solution(1537536714810398697)
XLA Ops:
  6.6 0.7 all-gather.2.cloned.1.call-update
  7.3 0.3 copy-done
  7.6 0.3 copy-done.1
  7.9 0.3 convolution_convert_fusion
  8.3 0.2 convolution_convert_fusion.4
  8.4 0.1 fusion.19
  8.6 7.0 %collective-permute-start.4 = (bf16[2,64,128]{2,1,0:T(8,128)(2,1)S(1)}, bf16[2,64,128]{2,1,0:T(8,128)(2,1)S(1)}, u32[]{:S(2)}, u32[]{:S(2)}) collective-permute-start(bf16[2,64,128]{2,1,0:T(8,128)(2,1)S(1)} %fusion.19), channel_id=1, source_target_pairs={{0,30},{2,0},{4,2},{6,4},{8,6},{10,8},{12,10},{14,12},{16,14},{18,... | collective-permute-start | bytes 98312 | tf_op jit(solution)/shard_map/ppermute | solution.py:20
  15.6 1.3 collective-permute-start.2
  16.9 1.3 collective-permute-start.3
  18.2 1.1 fusion.91
  19.2 5.3 %collective-permute-start = (bf16[2048,128]{1,0:T(8,128)(2,1)}, bf16[2048,128]{1,0:T(8,128)(2,1)}, u32[]{:S(2)}, u32[]{:S(2)}) collective-permute-start(bf16[2048,128]{1,0:T(8,128)(2,1)} %get-tuple-element.5), channel_id=1, source_target_pairs={{0,2},{2,4},{4,6},{6,8},{8,10},{10,12},{12,14},{14,16},{16,18},{18... | collective-permute-start | bytes 1572872 | tf_op jit(solution)/shard_map/ppermute | solution.py:33
  24.7 0.1 reshape.160
  24.9 0.1 reshape.152
  25.3 0.2 fusion.50
  25.5 49.3 %all_gather.7 = bf16[32,64,128]{2,1,0:T(8,128)(2,1)S(1)} all-gather(bf16[2,64,128]{2,1,0:T(8,128)(2,1)S(1)} %bitcast.104), channel_id=1, replica_groups=mesh['leaf'=16,'col'=2] {'leaf'}, dimensions={0}, use_global_device_ids=true | all-gather | bytes 557056 | tf_op jit(solution)/shard_map/all_gather | solution.py:88
  74.9 0.4 convolution_convert_fusion.1
  75.6 0.7 broadcast_in_dim.60
  76.3 0.7 copy.61
  76.9 1.2 gather_fusion.2
  78.1 1.3 collective-permute-start.1
  79.4 2.7 %collective-permute-start.7 = (bf16[2,64,128]{2,1,0:T(8,128)(2,1)S(1)}, bf16[2,64,128]{2,1,0:T(8,128)(2,1)S(1)}, u32[]{:S(2)}, u32[]{:S(2)}) collective-permute-start(bf16[2,64,128]{2,1,0:T(8,128)(2,1)S(1)} %collective-permute-done.5), channel_id=1, source_target_pairs={{0,2},{2,4},{4,6},{6,8},{8,10},{10,12},{12,14},{14,16},{16,18},{18... | collective-permute-start | bytes 98312 | tf_op jit(solution)/shard_map/ppermute | solution.py:18
  82.1 0.2 convolution_add_fusion.8
  82.3 0.2 convolution_add_fusion.7
  82.6 4.5 %collective-permute-done.7 = bf16[2,64,128]{2,1,0:T(8,128)(2,1)S(1)} collective-permute-done((bf16[2,64,128]{2,1,0:T(8,128)(2,1)S(1)}, bf16[2,64,128]{2,1,0:T(8,128)(2,1)S(1)}, u32[]{:S(2)}, u32[]{:S(2)}) %collective-permute-start.7) | collective-permute-done | bytes 32800 | tf_op jit(solution)/shard_map/ppermute | solution.py:18
  87.1 1.3 collective-permute-start.6
  88.4 0.2 fusion.45
  88.7 3.1 %collective-permute-done.6 = bf16[2,64,128]{2,1,0:T(8,128)(2,1)S(1)} collective-permute-done((bf16[2,64,128]{2,1,0:T(8,128)(2,1)S(1)}, bf16[2,64,128]{2,1,0:T(8,128)(2,1)S(1)}, u32[]{:S(2)}, u32[]{:S(2)}) %collective-permute-start.6) | collective-permute-done | bytes 32800 | tf_op jit(solution)/shard_map/ppermute | solution.py:20
  91.8 3.4 %collective-permute-start.9 = (bf16[2,64,128]{2,1,0:T(8,128)(2,1)S(1)}, bf16[2,64,128]{2,1,0:T(8,128)(2,1)S(1)}, u32[]{:S(2)}, u32[]{:S(2)}) collective-permute-start(bf16[2,64,128]{2,1,0:T(8,128)(2,1)S(1)} %collective-permute-done.7), channel_id=1, source_target_pairs={{0,2},{2,4},{4,6},{6,8},{8,10},{10,12},{12,14},{14,16},{16,18},{18... | collective-permute-start | bytes 98312 | tf_op jit(solution)/shard_map/ppermute | solution.py:18
  95.2 0.2 fusion.15
  95.4 3.9 %collective-permute-done.9 = bf16[2,64,128]{2,1,0:T(8,128)(2,1)S(1)} collective-permute-done((bf16[2,64,128]{2,1,0:T(8,128)(2,1)S(1)}, bf16[2,64,128]{2,1,0:T(8,128)(2,1)S(1)}, u32[]{:S(2)}, u32[]{:S(2)}) %collective-permute-start.9) | collective-permute-done | bytes 32800 | tf_op jit(solution)/shard_map/ppermute | solution.py:18
  99.3 0.6 collective-permute-start.8
  99.9 0.2 fusion.42
  100.1 3.1 %collective-permute-done.8 = bf16[2,64,128]{2,1,0:T(8,128)(2,1)S(1)} collective-permute-done((bf16[2,64,128]{2,1,0:T(8,128)(2,1)S(1)}, bf16[2,64,128]{2,1,0:T(8,128)(2,1)S(1)}, u32[]{:S(2)}, u32[]{:S(2)}) %collective-permute-start.8) | collective-permute-done | bytes 32800 | tf_op jit(solution)/shard_map/ppermute | solution.py:20
  103.2 0.7 collective-permute-start.11
  103.9 0.2 fusion.14
  104.1 6.7 %collective-permute-done.11 = bf16[2,64,128]{2,1,0:T(8,128)(2,1)} collective-permute-done((bf16[2,64,128]{2,1,0:T(8,128)(2,1)S(1)}, bf16[2,64,128]{2,1,0:T(8,128)(2,1)}, u32[]{:S(2)}, u32[]{:S(2)}) %collective-permute-start.11) | collective-permute-done | bytes 32800 | tf_op jit(solution)/shard_map/ppermute | solution.py:18
  110.8 0.8 collective-permute-start.10
  111.6 1.0 fusion.39
  112.6 2.3 %collective-permute-done.10 = bf16[2,64,128]{2,1,0:T(8,128)(2,1)} collective-permute-done((bf16[2,64,128]{2,1,0:T(8,128)(2,1)S(1)}, bf16[2,64,128]{2,1,0:T(8,128)(2,1)}, u32[]{:S(2)}, u32[]{:S(2)}) %collective-permute-start.10) | collective-permute-done | bytes 32800 | tf_op jit(solution)/shard_map/ppermute | solution.py:20
  114.8 1.0 fusion.13
  115.9 5.7 %collective-permute-start.12 = (bf16[2,64,128]{2,1,0:T(8,128)(2,1)}, bf16[2,64,128]{2,1,0:T(8,128)(2,1)S(1)}, u32[]{:S(2)}, u32[]{:S(2)}) collective-permute-start(bf16[2,64,128]{2,1,0:T(8,128)(2,1)} %collective-permute-done.10), channel_id=1, source_target_pairs={{0,30},{2,0},{4,2},{6,4},{8,6},{10,8},{12,10},{14,12},{16,14},{18,... | collective-permute-start | bytes 98312 | tf_op jit(solution)/shard_map/ppermute | solution.py:20
  121.5 1.0 pad_maximum_fusion.1
  122.6 0.7 gather_fusion.1
  123.4 5.8 %collective-permute-start.14 = (bf16[2,64,128]{2,1,0:T(8,128)(2,1)S(1)}, bf16[2,64,128]{2,1,0:T(8,128)(2,1)S(1)}, u32[]{:S(2)}, u32[]{:S(2)}) collective-permute-start(bf16[2,64,128]{2,1,0:T(8,128)(2,1)S(1)} %collective-permute-done.12), channel_id=1, source_target_pairs={{0,30},{2,0},{4,2},{6,4},{8,6},{10,8},{12,10},{14,12},{16,14},{18,... | collective-permute-start | bytes 98312 | tf_op jit(solution)/shard_map/ppermute | solution.py:20
  129.3 1.0 fusion.36
  130.2 0.2 fusion.12
  130.5 0.6 collective-permute-done.15
  131.1 5.6 %collective-permute-start.16 = (bf16[2,64,128]{2,1,0:T(8,128)(2,1)S(1)}, bf16[2,64,128]{2,1,0:T(8,128)(2,1)S(1)}, u32[]{:S(2)}, u32[]{:S(2)}) collective-permute-start(bf16[2,64,128]{2,1,0:T(8,128)(2,1)S(1)} %collective-permute-done.14), channel_id=1, source_target_pairs={{0,30},{2,0},{4,2},{6,4},{8,6},{10,8},{12,10},{14,12},{16,14},{18,... | collective-permute-start | bytes 98312 | tf_op jit(solution)/shard_map/ppermute | solution.py:20
  136.8 0.2 fusion.33
  137.0 0.2 fusion.11
  137.2 1.4 collective-permute-done.17
  138.6 0.2 fusion.30
  138.9 0.2 fusion.10
  139.1 7.0 %collective-permute-done.18 = bf16[2,64,128]{2,1,0:T(8,128)(2,1)S(1)} collective-permute-done((bf16[2,64,128]{2,1,0:T(8,128)(2,1)S(1)}, bf16[2,64,128]{2,1,0:T(8,128)(2,1)S(1)}, u32[]{:S(2)}, u32[]{:S(2)}) %collective-permute-start.18) | collective-permute-done | bytes 32800 | tf_op jit(solution)/shard_map/ppermute | solution.py:18
  146.1 0.2 fusion.16
  146.4 1.2 fusion.18
  147.7 1.2 convolution_bitcast_fusion.1
  148.9 0.2 copy.80
  149.1 1.9 fusion.9
  151.1 1.7 pad_maximum_fusion
  152.7 6.6 %gather_fusion = bf16[128,256,128]{2,1,0:T(8,128)(2,1)} fusion(bf16[32,256,128]{2,1,0:T(8,128)(2,1)S(1)} %bitcast.97, s32[1024]{0:T(1024)S(1)} %pad_clamp_fusion.2), kind=kCustom, calls=%fused_computation | custom fusion | bytes 16777728 | tf_op jit(solution)/shard_map/gather | solution.py:69
  159.3 12.1 %copy.58 = bf16[128,256,128]{1,2,0:T(8,128)(2,1)} copy(bf16[128,256,128]{2,1,0:T(8,128)(2,1)} %gather_fusion) | data formatting | bytes 16777216 | tf_op jit(solution)/shard_map/gather | solution.py:69
  171.4 12.7 %fusion.4 = f32[16,256,128]{1,2,0:T(8,128)} fusion(f32[16,128,256]{2,1,0:T(8,128)S(1)} %copy-done.2, bf16[16,8,256,256]{3,2,1,0:T(8,128)(2,1)} %all-gather.2.cloned.1.call-done, bf16[16,8,256,128]{2,3,1,0:T(8,128)(2,1)} %bitcast.99, pred[16,8]{1,0:T(8,128)(4,1)S(1)} %iota_compare_fusion.1), kind=kOutput, calls=%fused_computation.9 | convolution fusion | flops 2152202240 | bytes 29360256 | tf_op jit(solution)/shard_map/lsij,lsjc->lic/dot_general | solution.py:72
  184.1 2.9 %copy.81 = f32[16,256,128]{2,1,0:T(8,128)} copy(f32[16,256,128]{1,2,0:T(8,128)} %fusion.4) | data formatting | bytes 4194304 | tf_op jit(solution)/shard_map/add | solution.py:133
  (58 shorter events, 0.8 us)
Async XLA Ops:
  6.5 1.0 copy-start
  6.5 1.4 copy-start.1
  6.5 1.7 copy-start.4
  6.5 1.9 copy-start.7
  6.5 164.9 %all-gather.2.cloned.1.call-start = ((), (), s32[]{:S(2)}) async-start(), calls=%async_computation | async-start | bytes 25165824 | tf_op jit(solution)/shard_map/all_gather | solution.py:66
  7.3 17.3 %copy-start.12 = (s32[2,4]{1,0:T(2,128)S(1)}, s32[2,4]{1,0:T(2,128)}, u32[]{:S(2)}) copy-start(s32[2,4]{1,0:T(2,128)} %param.21) | copy-start | bytes 100
  7.3 17.4 %copy-start.10 = (s32[16,4]{0,1:T(4,128)S(1)}, s32[16,4]{0,1:T(4,128)}, u32[]{:S(2)}) copy-start(s32[16,4]{0,1:T(4,128)} %param.18) | copy-start | bytes 772
  7.3 17.5 %copy-start.9 = (s32[16,8]{0,1:T(8,128)S(1)}, s32[16,8]{0,1:T(8,128)}, u32[]{:S(2)}) copy-start(s32[16,8]{0,1:T(8,128)} %param.14) | copy-start | bytes 1540
  7.3 17.9 %copy-start.11 = (s32[16]{0:T(128)S(1)}, s32[16]{0:T(128)}, u32[]{:S(2)}) copy-start(s32[16]{0:T(128)} %param.15) | copy-start | bytes 196
  7.3 69.6 %copy-start.8 = (bf16[4,64,256]{2,1,0:T(8,128)(2,1)S(1)}, bf16[4,64,256]{2,1,0:T(8,128)(2,1)}, u32[]{:S(2)}) copy-start(bf16[4,64,256]{2,1,0:T(8,128)(2,1)} %param.23) | copy-start | bytes 393220
  8.6 69.5 %collective-permute-start.4 = (bf16[2,64,128]{2,1,0:T(8,128)(2,1)S(1)}, bf16[2,64,128]{2,1,0:T(8,128)(2,1)S(1)}, u32[]{:S(2)}, u32[]{:S(2)}) collective-permute-start(bf16[2,64,128]{2,1,0:T(8,128)(2,1)S(1)} %fusion.19), channel_id=1, source_target_pairs={{0,30},{2,0},{4,2},{6,4},{8,6},{10,8},{12,10},{14,12},{16,14},{18,... | collective-permute-start | bytes 98312 | tf_op jit(solution)/shard_map/ppermute | solution.py:20
  15.5 63.9 %collective-permute-start.5 = (bf16[2,64,128]{2,1,0:T(8,128)(2,1)S(1)}, bf16[2,64,128]{2,1,0:T(8,128)(2,1)S(1)}, u32[]{:S(2)}, u32[]{:S(2)}) collective-permute-start(bf16[2,64,128]{2,1,0:T(8,128)(2,1)S(1)} %fusion.19), channel_id=1, source_target_pairs={{0,2},{2,4},{4,6},{6,8},{8,10},{10,12},{12,14},{14,16},{16,18},{18... | collective-permute-start | bytes 98312 | tf_op jit(solution)/shard_map/ppermute | solution.py:18
  15.6 100.3 %collective-permute-start.2 = (bf16[8,64,128]{2,1,0:T(8,128)(2,1)S(1)}, bf16[8,64,128]{2,1,0:T(8,128)(2,1)S(1)}, u32[]{:S(2)}, u32[]{:S(2)}) collective-permute-start(bf16[8,64,128]{2,1,0:T(8,128)(2,1)S(1)} %get-tuple-element.7), channel_id=1, source_target_pairs={{0,2},{2,4},{4,6},{6,8},{8,10},{10,12},{12,14},{14,16},{16,18},{18... | collective-permute-start | bytes 393224 | tf_op jit(solution)/shard_map/ppermute | solution.py:33
  16.9 104.7 %collective-permute-start.3 = (bf16[8,64,128]{2,1,0:T(8,128)(2,1)S(1)}, bf16[8,64,128]{2,1,0:T(8,128)(2,1)}, u32[]{:S(2)}, u32[]{:S(2)}) collective-permute-start(bf16[8,64,128]{2,1,0:T(8,128)(2,1)S(1)} %get-tuple-element.8), channel_id=1, source_target_pairs={{2,0},{4,2},{6,4},{8,6},{10,8},{12,10},{14,12},{16,14},{18,16},{20... | collective-permute-start | bytes 393224 | tf_op jit(solution)/shard_map/ppermute | solution.py:34
  19.2 131.8 %collective-permute-start = (bf16[2048,128]{1,0:T(8,128)(2,1)}, bf16[2048,128]{1,0:T(8,128)(2,1)}, u32[]{:S(2)}, u32[]{:S(2)}) collective-permute-start(bf16[2048,128]{1,0:T(8,128)(2,1)} %get-tuple-element.5), channel_id=1, source_target_pairs={{0,2},{2,4},{4,6},{6,8},{8,10},{10,12},{12,14},{14,16},{16,18},{18... | collective-permute-start | bytes 1572872 | tf_op jit(solution)/shard_map/ppermute | solution.py:33
  78.1 72.9 %collective-permute-start.1 = (bf16[2048,128]{1,0:T(8,128)(2,1)}, bf16[2048,128]{1,0:T(8,128)(2,1)}, u32[]{:S(2)}, u32[]{:S(2)}) collective-permute-start(bf16[2048,128]{1,0:T(8,128)(2,1)} %get-tuple-element.6), channel_id=1, source_target_pairs={{2,0},{4,2},{6,4},{8,6},{10,8},{12,10},{14,12},{16,14},{18,16},{20... | collective-permute-start | bytes 1572872 | tf_op jit(solution)/shard_map/ppermute | solution.py:34
  79.4 7.7 %collective-permute-start.7 = (bf16[2,64,128]{2,1,0:T(8,128)(2,1)S(1)}, bf16[2,64,128]{2,1,0:T(8,128)(2,1)S(1)}, u32[]{:S(2)}, u32[]{:S(2)}) collective-permute-start(bf16[2,64,128]{2,1,0:T(8,128)(2,1)S(1)} %collective-permute-done.5), channel_id=1, source_target_pairs={{0,2},{2,4},{4,6},{6,8},{8,10},{10,12},{12,14},{14,16},{16,18},{18... | collective-permute-start | bytes 98312 | tf_op jit(solution)/shard_map/ppermute | solution.py:18
  87.1 4.6 %collective-permute-start.6 = (bf16[2,64,128]{2,1,0:T(8,128)(2,1)S(1)}, bf16[2,64,128]{2,1,0:T(8,128)(2,1)S(1)}, u32[]{:S(2)}, u32[]{:S(2)}) collective-permute-start(bf16[2,64,128]{2,1,0:T(8,128)(2,1)S(1)} %collective-permute-done.4), channel_id=1, source_target_pairs={{0,30},{2,0},{4,2},{6,4},{8,6},{10,8},{12,10},{14,12},{16,14},{18,... | collective-permute-start | bytes 98312 | tf_op jit(solution)/shard_map/ppermute | solution.py:20
  91.8 7.5 %collective-permute-start.9 = (bf16[2,64,128]{2,1,0:T(8,128)(2,1)S(1)}, bf16[2,64,128]{2,1,0:T(8,128)(2,1)S(1)}, u32[]{:S(2)}, u32[]{:S(2)}) collective-permute-start(bf16[2,64,128]{2,1,0:T(8,128)(2,1)S(1)} %collective-permute-done.7), channel_id=1, source_target_pairs={{0,2},{2,4},{4,6},{6,8},{8,10},{10,12},{12,14},{14,16},{16,18},{18... | collective-permute-start | bytes 98312 | tf_op jit(solution)/shard_map/ppermute | solution.py:18
  99.3 3.9 %collective-permute-start.8 = (bf16[2,64,128]{2,1,0:T(8,128)(2,1)S(1)}, bf16[2,64,128]{2,1,0:T(8,128)(2,1)S(1)}, u32[]{:S(2)}, u32[]{:S(2)}) collective-permute-start(bf16[2,64,128]{2,1,0:T(8,128)(2,1)S(1)} %collective-permute-done.6), channel_id=1, source_target_pairs={{0,30},{2,0},{4,2},{6,4},{8,6},{10,8},{12,10},{14,12},{16,14},{18,... | collective-permute-start | bytes 98312 | tf_op jit(solution)/shard_map/ppermute | solution.py:20
  100.1 49.0 %copy-start.3 = (bf16[16,64,256]{2,1,0:T(8,128)(2,1)S(1)}, bf16[16,64,256]{2,1,0:T(8,128)(2,1)}, u32[]{:S(2)}) copy-start(bf16[16,64,256]{2,1,0:T(8,128)(2,1)} %param.17) | copy-start | bytes 1572868
  103.2 7.6 %collective-permute-start.11 = (bf16[2,64,128]{2,1,0:T(8,128)(2,1)S(1)}, bf16[2,64,128]{2,1,0:T(8,128)(2,1)}, u32[]{:S(2)}, u32[]{:S(2)}) collective-permute-start(bf16[2,64,128]{2,1,0:T(8,128)(2,1)S(1)} %collective-permute-done.9), channel_id=1, source_target_pairs={{0,2},{2,4},{4,6},{6,8},{8,10},{10,12},{12,14},{14,16},{16,18},{18... | collective-permute-start | bytes 98312 | tf_op jit(solution)/shard_map/ppermute | solution.py:18
  110.8 4.0 %collective-permute-start.10 = (bf16[2,64,128]{2,1,0:T(8,128)(2,1)S(1)}, bf16[2,64,128]{2,1,0:T(8,128)(2,1)}, u32[]{:S(2)}, u32[]{:S(2)}) collective-permute-start(bf16[2,64,128]{2,1,0:T(8,128)(2,1)S(1)} %collective-permute-done.8), channel_id=1, source_target_pairs={{0,30},{2,0},{4,2},{6,4},{8,6},{10,8},{12,10},{14,12},{16,14},{18,... | collective-permute-start | bytes 98312 | tf_op jit(solution)/shard_map/ppermute | solution.py:20
  114.8 8.5 %collective-permute-start.13 = (bf16[2,64,128]{2,1,0:T(8,128)(2,1)}, bf16[2,64,128]{2,1,0:T(8,128)(2,1)}, u32[]{:S(2)}, u32[]{:S(2)}) collective-permute-start(bf16[2,64,128]{2,1,0:T(8,128)(2,1)} %collective-permute-done.11), channel_id=1, source_target_pairs={{0,2},{2,4},{4,6},{6,8},{8,10},{10,12},{12,14},{14,16},{16,18},{18... | collective-permute-start | bytes 98312 | tf_op jit(solution)/shard_map/ppermute | solution.py:18
  115.8 5.7 %copy-start.6 = (bf16[8,64,128]{2,1,0:T(8,128)(2,1)}, bf16[8,64,128]{2,1,0:T(8,128)(2,1)S(1)}, u32[]{:S(2)}) copy-start(bf16[8,64,128]{2,1,0:T(8,128)(2,1)S(1)} %collective-permute-done.2) | copy-start | bytes 393220
  115.9 7.6 %collective-permute-start.12 = (bf16[2,64,128]{2,1,0:T(8,128)(2,1)}, bf16[2,64,128]{2,1,0:T(8,128)(2,1)S(1)}, u32[]{:S(2)}, u32[]{:S(2)}) collective-permute-start(bf16[2,64,128]{2,1,0:T(8,128)(2,1)} %collective-permute-done.10), channel_id=1, source_target_pairs={{0,30},{2,0},{4,2},{6,4},{8,6},{10,8},{12,10},{14,12},{16,14},{18,... | collective-permute-start | bytes 98312 | tf_op jit(solution)/shard_map/ppermute | solution.py:20
  122.6 25.1 %copy-start.5 = (bf16[8,64,128]{2,1,0:T(8,128)(2,1)S(1)}, bf16[8,64,128]{2,1,0:T(8,128)(2,1)}, u32[]{:S(2)}) copy-start(bf16[8,64,128]{2,1,0:T(8,128)(2,1)} %copy.61) | copy-start | bytes 393220
  123.3 7.8 %collective-permute-start.15 = (bf16[2,64,128]{2,1,0:T(8,128)(2,1)}, bf16[2,64,128]{2,1,0:T(8,128)(2,1)S(1)}, u32[]{:S(2)}, u32[]{:S(2)}) collective-permute-start(bf16[2,64,128]{2,1,0:T(8,128)(2,1)} %collective-permute-done.13), channel_id=1, source_target_pairs={{0,2},{2,4},{4,6},{6,8},{8,10},{10,12},{12,14},{14,16},{16,18},{18... | collective-permute-start | bytes 98312 | tf_op jit(solution)/shard_map/ppermute | solution.py:18
  123.4 7.7 %collective-permute-start.14 = (bf16[2,64,128]{2,1,0:T(8,128)(2,1)S(1)}, bf16[2,64,128]{2,1,0:T(8,128)(2,1)S(1)}, u32[]{:S(2)}, u32[]{:S(2)}) collective-permute-start(bf16[2,64,128]{2,1,0:T(8,128)(2,1)S(1)} %collective-permute-done.12), channel_id=1, source_target_pairs={{0,30},{2,0},{4,2},{6,4},{8,6},{10,8},{12,10},{14,12},{16,14},{18,... | collective-permute-start | bytes 98312 | tf_op jit(solution)/shard_map/ppermute | solution.py:20
  131.1 7.5 %collective-permute-start.17 = (bf16[2,64,128]{2,1,0:T(8,128)(2,1)S(1)}, bf16[2,64,128]{2,1,0:T(8,128)(2,1)S(1)}, u32[]{:S(2)}, u32[]{:S(2)}) collective-permute-start(bf16[2,64,128]{2,1,0:T(8,128)(2,1)S(1)} %collective-permute-done.15), channel_id=1, source_target_pairs={{0,2},{2,4},{4,6},{6,8},{8,10},{10,12},{12,14},{14,16},{16,18},{18... | collective-permute-start | bytes 98312 | tf_op jit(solution)/shard_map/ppermute | solution.py:18
  131.1 7.7 %collective-permute-start.16 = (bf16[2,64,128]{2,1,0:T(8,128)(2,1)S(1)}, bf16[2,64,128]{2,1,0:T(8,128)(2,1)S(1)}, u32[]{:S(2)}, u32[]{:S(2)}) collective-permute-start(bf16[2,64,128]{2,1,0:T(8,128)(2,1)S(1)} %collective-permute-done.14), channel_id=1, source_target_pairs={{0,30},{2,0},{4,2},{6,4},{8,6},{10,8},{12,10},{14,12},{16,14},{18,... | collective-permute-start | bytes 98312 | tf_op jit(solution)/shard_map/ppermute | solution.py:20
  138.6 7.5 %collective-permute-start.18 = (bf16[2,64,128]{2,1,0:T(8,128)(2,1)S(1)}, bf16[2,64,128]{2,1,0:T(8,128)(2,1)S(1)}, u32[]{:S(2)}, u32[]{:S(2)}) collective-permute-start(bf16[2,64,128]{2,1,0:T(8,128)(2,1)S(1)} %collective-permute-done.17), channel_id=1, source_target_pairs={{0,2},{2,4},{4,6},{6,8},{8,10},{10,12},{12,14},{14,16},{16,18},{18... | collective-permute-start | bytes 98312 | tf_op jit(solution)/shard_map/ppermute | solution.py:18
  159.3 12.1 %copy-start.2 = (f32[16,128,256]{2,1,0:T(8,128)S(1)}, f32[16,128,256]{2,1,0:T(8,128)}, u32[]{:S(2)}) copy-start(f32[16,128,256]{2,1,0:T(8,128)} %fusion.9) | copy-start | bytes 6291460
Sparse Core Ops, SparseCore 0:
  8.9 32.7 all-gather.1
